TPU v7x, 32 devices: a whole 2x2x4 slice. The times are simulated.
32 devices in a mesh: subtree: 4 (over y, core), tile: 8 (over z, x).
Axes of the slice: x: 2, y: 2, z: 4, core: 2. Of those that a mesh axis runs over, the one named last changes fastest.
Arguments:
- interface_stiffness: float32 [4, 4096, 4096], P('subtree', 'tile'), may hold values from -3 to 3
- lower_factor: bfloat16 [4, 4096, 512], P('subtree', 'tile'), may hold values from -0.25 to 0.25
- upper_factor: bfloat16 [4, 512, 4096], P('subtree', None, 'tile'), may hold values from -6 to 6
- modes: bfloat16 [4096, 256], P('tile'), may hold values from -0.09375 to 0.09375
- gyro_rows: int32 [512], replicated, may hold values from 0 to 4095, as said below
- gyro_coupling: float32 [512, 512], replicated, may hold values from -24 to 24
- spin_softening: float32 [512], replicated, may hold values from 0.5 to 8
- speed_index: int32 [2], replicated, may hold values from 0 to 63
Outputs:
- schur: float32 [4096, 4096], P('tile', 'subtree')
- campbell: float32 [2, 256, 256], P(None, 'tile', 'subtree')
Inputs may be any that keep to these rules, and one draw needn't show every extreme that they name: `gyro_rows`: distinct interface degrees of freedom, in whole aligned blocks of 8 consecutive ones.
All inputs are finite; a program needn't handle non-finite values.
Results may differ from a plain program's by a relative error of at most 0.0003.
Values may be sent and summed in bfloat16 or wider, within the bound.
No kernel may reach another device: no remote copies, remote signals or barrier semaphores. Data moves between devices by JAX's collectives and lax.ppermute only.
A program may use at most 64 MiB of HBM per device.

v0:
```python
import jax
import jax.numpy as jnp
from jax import lax
from jax.sharding import PartitionSpec as P

SPEED_STEPS = 64
OMEGA_TOP = 2.0


def partner(block, axis, distance):
    count = lax.axis_size(axis)
    route = []
    for low in range(count):
        high = low | 1 << distance
        if high != low and high < count:
            route += [(low, high), (high, low)]
    return lax.ppermute(block, axis, route)


def shards(
    interface_stiffness,
    lower_factor,
    upper_factor,
    modes,
    gyro_rows,
    gyro_coupling,
    spin_softening,
    speed_index,
):
    tile_count = lax.axis_size("tile")
    branch_count = lax.axis_size("subtree")
    tile_pos = lax.axis_index("tile")
    branch_pos = lax.axis_index("subtree")
    mode_count = modes.shape[1]
    mode_cols = mode_count // branch_count
    mode_rows_dev = mode_count // tile_count
    coupled = jnp.einsum(
        "lrk,lkn->rn",
        lower_factor,
        lax.all_gather(upper_factor, "tile", axis=2, tiled=True),
        preferred_element_type=jnp.float32,
    )
    schur_rows = jnp.sum(interface_stiffness, axis=0) - coupled
    full_width = schur_rows.shape[1]
    own_width = full_width // branch_count
    own_first = branch_pos * own_width
    schur_part = schur_rows
    for level_bit in range(branch_count.bit_length() - 1):
        schur_part = schur_part + partner(schur_part, "subtree", level_bit)
    schur_out = lax.dynamic_slice_in_dim(schur_part, own_first, own_width, 1)
    col_first = branch_pos * mode_cols
    segment = lax.all_gather(modes, "tile", axis=0, tiled=True)
    row_count = segment.shape[0]
    wanted = lax.dynamic_slice_in_dim(segment, col_first, mode_cols, 1).astype(jnp.float32)
    response = jnp.dot(
        schur_part, wanted, precision=lax.Precision.HIGHEST, preferred_element_type=jnp.float32
    )
    inside = (gyro_rows >= 0) & (gyro_rows < row_count)
    taken = jnp.take(segment, jnp.clip(gyro_rows, 0, row_count - 1), axis=0).astype(jnp.float32)
    picked = jnp.where(inside[:, None], taken, jnp.float32(0.0))
    response, picked = (response, picked)
    local_modes = modes.astype(jnp.float32)
    partial_value = jnp.einsum(
        "rm,rc->mc",
        local_modes,
        response,
        precision=lax.Precision.HIGHEST,
        preferred_element_type=jnp.float32,
    )
    stiff_block = lax.psum_scatter(partial_value, "tile", scatter_dimension=0, tiled=True)
    skew_part = 0.5 * (gyro_coupling - gyro_coupling.T)
    left_modes = lax.dynamic_slice_in_dim(picked, tile_pos * mode_rows_dev, mode_rows_dev, 1)
    right_modes = lax.dynamic_slice_in_dim(picked, branch_pos * mode_cols, mode_cols, 1)
    turned = jnp.dot(
        skew_part, right_modes, precision=lax.Precision.HIGHEST, preferred_element_type=jnp.float32
    )
    gyro_block = jnp.einsum(
        "gm,gc->mc",
        left_modes,
        turned,
        precision=lax.Precision.HIGHEST,
        preferred_element_type=jnp.float32,
    )
    spin_block = jnp.einsum(
        "gm,gc->mc",
        left_modes,
        spin_softening[:, None] * right_modes,
        precision=lax.Precision.HIGHEST,
        preferred_element_type=jnp.float32,
    )
    speeds_omega = OMEGA_TOP * (speed_index.astype(jnp.float32) + 1.0) / SPEED_STEPS
    campbell = (
        stiff_block[None]
        + speeds_omega[:, None, None] * gyro_block[None]
        - (speeds_omega * speeds_omega)[:, None, None] * spin_block[None]
    )
    return (schur_out, campbell)


def solution(mesh):
    placed = (
        P("subtree", "tile", None),
        P("subtree", "tile", None),
        P("subtree", None, "tile"),
        P("tile", None),
        P(),
        P(),
        P(),
        P(),
    )
    return jax.shard_map(
        shards,
        mesh=mesh,
        in_specs=placed,
        out_specs=(P("tile", "subtree"), P(None, "tile", "subtree")),
        check_vma=False,
    )
```

profile of v0, /device:TPU:0, one launch (start us, length us, event | category | flops | bytes accessed | tf_op | source)
XLA Modules:
  0.0 391.6 jit_solution(2700897672948704366)
XLA Ops:
  7.2 0.7 all-gather.3.cloned.1.call-update
  8.0 79.8 %all-gather.3.cloned.1.call-done = bf16[1,512,4096]{2,1,0:T(8,128)(2,1)} async-done(((bf16[1,512,512]{2,1,0:T(8,128)(2,1)}), bf16[1,512,4096]{2,1,0:T(8,128)(2,1)}) %all-gather.3.cloned.1.call-update) | async-done | bytes 4194320 | tf_op jit(solution)/shard_map/all_gather | solution.py:40
  87.8 7.0 %bitcast_subtract_fusion = f32[512,4096]{1,0:T(8,128)S(1)} fusion(f32[1,512,4096]{2,1,0:T(8,128)} %param.8, bf16[1,512,4096]{2,1,0:T(8,128)(2,1)} %all-gather.3.cloned.1.call-done, bf16[1,512,512]{2,1,0:T(8,128)(2,1)S(1)} %copy-done), kind=kOutput, calls=%fused_computation.1 | convolution fusion | flops 2149580800 | bytes 21495808 | tf_op jit(solution)/shard_map/lrk,lkn->rn/dot_general | solution.py:37
  94.8 3.2 copy-done.1
  98.1 0.1 collective-permute-start
  98.2 13.3 %collective-permute-done = f32[512,4096]{1,0:T(8,128)} collective-permute-done((f32[512,4096]{1,0:T(8,128)S(1)}, f32[512,4096]{1,0:T(8,128)}, u32[]{:S(2)}, u32[]{:S(2)}) %collective-permute-start) | collective-permute-done | bytes 8388640 | tf_op jit(solution)/shard_map/ppermute | solution.py:17
  111.4 11.1 %add.35 = f32[512,4096]{1,0:T(8,128)} add(f32[512,4096]{1,0:T(8,128)} %copy-done.1, f32[512,4096]{1,0:T(8,128)} %collective-permute-done) | non-fusion elementwise | flops 2097152 | bytes 25165824 | tf_op jit(solution)/shard_map/add | solution.py:49
  122.6 1.5 collective-permute-start.1
  124.1 0.0 reduce-scatter.4.cloned.1.call-start
  124.2 0.3 copy.13
  124.6 46.2 %all-gather.5.cloned.1.call-done = bf16[4096,256]{1,0:T(8,128)(2,1)} async-done(((bf16[512,256]{1,0:T(8,128)(2,1)}), bf16[4096,256]{1,0:T(8,128)(2,1)}) %all-gather.5.cloned.1.call-update) | async-done | bytes 2097168 | tf_op jit(solution)/shard_map/all_gather | solution.py:52
  170.8 3.4 gather_fusion
  174.2 0.2 convert_select_fusion
  174.4 0.8 fusion.8
  175.3 1.1 fusion.2
  176.4 0.7 fusion.13
  177.0 128.3 %collective-permute-done.1 = f32[512,4096]{1,0:T(8,128)} collective-permute-done((f32[512,4096]{1,0:T(8,128)}, f32[512,4096]{1,0:T(8,128)}, u32[]{:S(2)}, u32[]{:S(2)}) %collective-permute-start.1) | collective-permute-done | bytes 8388640 | tf_op jit(solution)/shard_map/ppermute | solution.py:17
  305.4 11.1 %add.36 = f32[512,4096]{1,0:T(8,128)} add(f32[512,4096]{1,0:T(8,128)} %add.35, f32[512,4096]{1,0:T(8,128)} %collective-permute-done.1) | non-fusion elementwise | flops 2097152 | bytes 25165824 | tf_op jit(solution)/shard_map/add | solution.py:49
  316.5 6.7 %fusion.4 = f32[512,64]{1,0:T(8,128)S(1)} fusion(f32[512,4096]{1,0:T(8,128)} %add.36, bf16[4096,256]{1,0:T(8,128)(2,1)S(1)} %copy-done.2, s32[]{:T(128)S(6)} %select_n.24), kind=kOutput, calls=%fused_computation.7 | convolution fusion | flops 1610612736 | bytes 9568260 | tf_op jit(solution)/shard_map/dot_general | solution.py:55
  323.3 0.4 convolution_bitcast_fusion
  323.6 0.8 copy.14
  324.4 3.2 constant_dynamic-slice_fusion
  327.6 56.0 %reduce-scatter.4.cloned.1.call-done = f32[32,64]{1,0:T(8,128)} async-done(((f32[256,64]{1,0:T(8,128)}), f32[32,64]{1,0:T(8,128)}) %reduce-scatter.4.cloned.1.call-update) | async-done | bytes 8208 | tf_op jit(solution)/shard_map/reduce_scatter | solution.py:70
  383.6 1.4 multiply_subtract_fusion
  (23 shorter events, 0.2 us)
Async XLA Ops:
  7.2 80.6 %copy-start = (bf16[1,512,512]{2,1,0:T(8,128)(2,1)S(1)}, bf16[1,512,512]{2,1,0:T(8,128)(2,1)}, u32[]{:S(2)}) copy-start(bf16[1,512,512]{2,1,0:T(8,128)(2,1)} %param.9) | copy-start | bytes 1572868
  7.2 80.6 %all-gather.3.cloned.1.call-start = ((), (), s32[]{:S(2)}) async-start(), calls=%async_computation.1 | async-start | bytes 4718592 | tf_op jit(solution)/shard_map/all_gather | solution.py:40
  7.9 162.9 %all-gather.5.cloned.1.call-start = ((), (), s32[]{:S(2)}) async-start(), calls=%async_computation.2 | async-start | bytes 2359296 | tf_op jit(solution)/shard_map/all_gather | solution.py:52
  94.8 3.2 copy-start.1
  98.1 26.1 %copy-start.3 = (f32[512,512]{1,0:T(8,128)S(1)}, f32[512,512]{1,0:T(8,128)}, u32[]{:S(2)}) copy-start(f32[512,512]{1,0:T(8,128)} %param.13) | copy-start | bytes 3145732
  98.1 26.4 %copy-start.5 = (s32[512]{0:T(512)S(1)}, s32[512]{0:T(512)}, u32[]{:S(2)}) copy-start(s32[512]{0:T(512)} %param.12) | copy-start | bytes 6148
  98.1 26.5 %copy-start.7 = (s32[2]{0:T(128)S(1)}, s32[2]{0:T(128)}, u32[]{:S(2)}) copy-start(s32[2]{0:T(128)} %param.15) | copy-start | bytes 28
  98.1 76.4 %copy-start.6 = (f32[512]{0:T(512)S(1)}, f32[512]{0:T(512)}, u32[]{:S(2)}) copy-start(f32[512]{0:T(512)} %param.14) | copy-start | bytes 6148
  98.1 13.4 %collective-permute-start = (f32[512,4096]{1,0:T(8,128)S(1)}, f32[512,4096]{1,0:T(8,128)}, u32[]{:S(2)}, u32[]{:S(2)}) collective-permute-start(f32[512,4096]{1,0:T(8,128)S(1)} %bitcast_subtract_fusion), channel_id=1, source_target_pairs={{0,8},{8,0},{16,24},{24,16},{1,9},{9,1},{17,25},{25,17},{2,10},{10... | collective-permute-start | bytes 25165832 | tf_op jit(solution)/shard_map/ppermute | solution.py:17
  122.6 182.8 %collective-permute-start.1 = (f32[512,4096]{1,0:T(8,128)}, f32[512,4096]{1,0:T(8,128)}, u32[]{:S(2)}, u32[]{:S(2)}) collective-permute-start(f32[512,4096]{1,0:T(8,128)} %add.35), channel_id=1, source_target_pairs={{0,16},{16,0},{8,24},{24,8},{1,17},{17,1},{9,25},{25,9},{2,18},{18... | collective-permute-start | bytes 25165832 | tf_op jit(solution)/shard_map/ppermute | solution.py:17
  124.1 259.5 %reduce-scatter.4.cloned.1.call-start = ((), (), s32[]{:S(2)}) async-start(), calls=%async_computation.3 | async-start | bytes 147456 | tf_op jit(solution)/shard_map/reduce_scatter | solution.py:70
  177.0 139.5 %copy-start.2 = (bf16[4096,256]{1,0:T(8,128)(2,1)S(1)}, bf16[4096,256]{1,0:T(8,128)(2,1)}, u32[]{:S(2)}) copy-start(bf16[4096,256]{1,0:T(8,128)(2,1)} %all-gather.5.cloned.1.call-done) | copy-start | bytes 6291460
  316.5 6.7 %copy-start.4 = (bf16[512,256]{1,0:T(8,128)(2,1)S(1)}, bf16[512,256]{1,0:T(8,128)(2,1)}, u32[]{:S(2)}) copy-start(bf16[512,256]{1,0:T(8,128)(2,1)} %param.11) | copy-start | bytes 786436
Sparse Core Ops, SparseCore 0:
  10.1 77.7 all-gather.2
  124.2 46.5 all-gather.4
  324.5 59.0 reduce-scatter.3
where the time goes:
time: 392 us
  waiting for transfers between devices  324 us (83%)
  other arithmetic  23.9 us (6%)
  matrix products  16.7 us (4%)
  between operations  13.9 us (4%)
  local copies, waits for them, and re-layouts  10.9 us (3%)
    ppermute x2, waiting for transfers between devices, partner(): return lax.ppermute(block, axis, route)  142 us
    all_gather x1, waiting for transfers between devices, shards(): lax.all_gather(upper_factor, 'tile', axis=2, tiled=True)  79.8 us
    reduce_scatter x1, waiting for transfers between devices, shards(): lax.psum_scatter(partial_value, 'tile', scatter_dimension=0, tiled=True)  56 us
    all_gather x1, waiting for transfers between devices, shards(): segment = lax.all_gather(modes, 'tile', axis=0, tiled=True)  46.2 us
    add x2, other arithmetic, shards(): schur_part = schur_part + partner(schur_part, 'subtree', level_bit)  22.3 us
  transfers between devices with their start and end apart: 5, of which 5 were waited for; matrix products, arithmetic and copies ran while one was open for 2% of the time, Pallas kernels for 0%

commit v1 on v0

--- a/solution.py
+++ b/solution.py
@@ -49,7 +49,12 @@
         schur_part = schur_part + partner(schur_part, "subtree", level_bit)
     schur_out = lax.dynamic_slice_in_dim(schur_part, own_first, own_width, 1)
     col_first = branch_pos * mode_cols
-    segment = lax.all_gather(modes, "tile", axis=0, tiled=True)
+    ring = [modes]
+    for hop in range(7):
+        ring.append(lax.ppermute(ring[-1], "tile", [(dev, (dev + 1) % 8) for dev in range(8)]))
+    segment = jnp.roll(
+        jnp.concatenate(ring[::-1], axis=0), (lax.axis_index("tile") + 1) * ring[0].shape[0], axis=0
+    )
     row_count = segment.shape[0]
     wanted = lax.dynamic_slice_in_dim(segment, col_first, mode_cols, 1).astype(jnp.float32)
     response = jnp.dot(

time: 392 us -> 393 us (level)
  waiting for transfers between devices: 324 us -> 319 us
    ppermute x0 -> x7, waiting for transfers between devices: none -> 64.3 us  [shards(): lax.ppermute(ring[-1], 'tile', [(dev, (dev + 1) % 8) for dev in range(8)])]
    all_gather x1 -> x0, waiting for transfers between devices: 46.2 us -> none  [shards(): segment = lax.all_gather(modes, 'tile', axis=0, tiled=True)]
    ppermute x2, waiting for transfers between devices: 142 us -> 119 us  [partner(): return lax.ppermute(block, axis, route)]
  transfers between devices with their start and end apart: 5 -> 11, of which waited for: 5 -> 11; matrix products, arithmetic and copies ran while one was open for 2% -> 3% of each run, Pallas kernels for 0% -> 0%
where the time goes in v1:
time: 393 us
  waiting for transfers between devices  319 us (81%)
  other arithmetic  24 us (6%)
  matrix products  19.6 us (5%)
  between operations  14.3 us (4%)
  local copies, waits for them, and re-layouts  12.8 us (3%)
    ppermute x2, waiting for transfers between devices, partner(): return lax.ppermute(block, axis, route)  119 us
    all_gather x1, waiting for transfers between devices, shards(): lax.all_gather(upper_factor, 'tile', axis=2, tiled=True)  79.8 us
    ppermute x7, waiting for transfers between devices, shards(): lax.ppermute(ring[-1], 'tile', [(dev, (dev + 1) % 8) for dev in range(8)])  64.3 us
    reduce_scatter x1, waiting for transfers between devices, shards(): lax.psum_scatter(partial_value, 'tile', scatter_dimension=0, tiled=True)  55.7 us
    add x2, other arithmetic, shards(): schur_part = schur_part + partner(schur_part, 'subtree', level_bit)  22.3 us
    dot_general x1, matrix products, shards(): jnp.dot(schur_part, wanted, precision=lax.Precision.HIGHEST, preferred_el...  8.09 us
  transfers between devices with their start and end apart: 11, of which 11 were waited for; matrix products, arithmetic and copies ran while one was open for 3% of the time, Pallas kernels for 0%

profile of v1, /device:TPU:0, one launch (start us, length us, event | category | flops | bytes accessed | tf_op | source)
XLA Modules:
  0.0 392.9 jit_solution(16566173384467039758)
XLA Ops:
  8.0 79.8 %all-gather.2.cloned.1.call-done = bf16[1,512,4096]{2,1,0:T(8,128)(2,1)} async-done(((bf16[1,512,512]{2,1,0:T(8,128)(2,1)}), bf16[1,512,4096]{2,1,0:T(8,128)(2,1)}) %all-gather.2.cloned.1.call-update) | async-done | bytes 4194320 | tf_op jit(solution)/shard_map/all_gather | solution.py:40
  87.8 7.0 %bitcast_subtract_fusion = f32[512,4096]{1,0:T(8,128)S(1)} fusion(f32[1,512,4096]{2,1,0:T(8,128)} %param.8, bf16[1,512,4096]{2,1,0:T(8,128)(2,1)} %all-gather.2.cloned.1.call-done, bf16[1,512,512]{2,1,0:T(8,128)(2,1)S(1)} %copy-done), kind=kOutput, calls=%fused_computation.1 | convolution fusion | flops 2149580800 | bytes 21495808 | tf_op jit(solution)/shard_map/lrk,lkn->rn/dot_general | solution.py:37
  94.8 3.2 copy-done.2
  98.1 13.3 %collective-permute-done = f32[512,4096]{1,0:T(8,128)} collective-permute-done((f32[512,4096]{1,0:T(8,128)S(1)}, f32[512,4096]{1,0:T(8,128)}, u32[]{:S(2)}, u32[]{:S(2)}) %collective-permute-start) | collective-permute-done | bytes 8388640 | tf_op jit(solution)/shard_map/ppermute | solution.py:17
  111.4 11.2 %add.50 = f32[512,4096]{1,0:T(8,128)} add(f32[512,4096]{1,0:T(8,128)} %copy-done.2, f32[512,4096]{1,0:T(8,128)} %collective-permute-done) | non-fusion elementwise | flops 2097152 | bytes 25165824 | tf_op jit(solution)/shard_map/add | solution.py:49
  122.6 1.5 collective-permute-start.1
  124.1 1.4 collective-permute-start.2
  125.5 9.3 %collective-permute-done.2 = bf16[512,256]{1,0:T(8,128)(2,1)S(1)} collective-permute-done((bf16[512,256]{1,0:T(8,128)(2,1)S(1)}, bf16[512,256]{1,0:T(8,128)(2,1)S(1)}, u32[]{:S(2)}, u32[]{:S(2)}) %collective-permute-start.2) | collective-permute-done | bytes 262176 | tf_op jit(solution)/shard_map/ppermute | solution.py:54
  134.8 9.9 %collective-permute-done.3 = bf16[512,256]{1,0:T(8,128)(2,1)S(1)} collective-permute-done((bf16[512,256]{1,0:T(8,128)(2,1)S(1)}, bf16[512,256]{1,0:T(8,128)(2,1)S(1)}, u32[]{:S(2)}, u32[]{:S(2)}) %collective-permute-start.3) | collective-permute-done | bytes 262176 | tf_op jit(solution)/shard_map/ppermute | solution.py:54
  144.7 9.1 %collective-permute-done.4 = bf16[512,256]{1,0:T(8,128)(2,1)S(1)} collective-permute-done((bf16[512,256]{1,0:T(8,128)(2,1)S(1)}, bf16[512,256]{1,0:T(8,128)(2,1)S(1)}, u32[]{:S(2)}, u32[]{:S(2)}) %collective-permute-start.4) | collective-permute-done | bytes 262176 | tf_op jit(solution)/shard_map/ppermute | solution.py:54
  153.8 9.1 %collective-permute-done.5 = bf16[512,256]{1,0:T(8,128)(2,1)S(1)} collective-permute-done((bf16[512,256]{1,0:T(8,128)(2,1)S(1)}, bf16[512,256]{1,0:T(8,128)(2,1)S(1)}, u32[]{:S(2)}, u32[]{:S(2)}) %collective-permute-start.5) | collective-permute-done | bytes 262176 | tf_op jit(solution)/shard_map/ppermute | solution.py:54
  162.9 9.1 %collective-permute-done.6 = bf16[512,256]{1,0:T(8,128)(2,1)S(1)} collective-permute-done((bf16[512,256]{1,0:T(8,128)(2,1)S(1)}, bf16[512,256]{1,0:T(8,128)(2,1)S(1)}, u32[]{:S(2)}, u32[]{:S(2)}) %collective-permute-start.6) | collective-permute-done | bytes 262176 | tf_op jit(solution)/shard_map/ppermute | solution.py:54
  172.0 10.1 %collective-permute-done.7 = bf16[512,256]{1,0:T(8,128)(2,1)S(1)} collective-permute-done((bf16[512,256]{1,0:T(8,128)(2,1)S(1)}, bf16[512,256]{1,0:T(8,128)(2,1)S(1)}, u32[]{:S(2)}, u32[]{:S(2)}) %collective-permute-start.7) | collective-permute-done | bytes 262176 | tf_op jit(solution)/shard_map/ppermute | solution.py:54
  182.2 1.3 copy.13
  183.5 7.7 %collective-permute-done.8 = bf16[512,256]{1,0:T(8,128)(2,1)S(1)} collective-permute-done((bf16[512,256]{1,0:T(8,128)(2,1)S(1)}, bf16[512,256]{1,0:T(8,128)(2,1)S(1)}, u32[]{:S(2)}, u32[]{:S(2)}) %collective-permute-start.8) | collective-permute-done | bytes 262176 | tf_op jit(solution)/shard_map/ppermute | solution.py:54
  191.7 1.9 copy-done.4
  193.7 2.0 gather_fusion
  196.7 2.6 fusion.2
  200.0 105.3 %collective-permute-done.1 = f32[512,4096]{1,0:T(8,128)} collective-permute-done((f32[512,4096]{1,0:T(8,128)}, f32[512,4096]{1,0:T(8,128)}, u32[]{:S(2)}, u32[]{:S(2)}) %collective-permute-start.1) | collective-permute-done | bytes 8388640 | tf_op jit(solution)/shard_map/ppermute | solution.py:17
  305.4 11.2 %add.51 = f32[512,4096]{1,0:T(8,128)} add(f32[512,4096]{1,0:T(8,128)} %add.50, f32[512,4096]{1,0:T(8,128)} %collective-permute-done.1) | non-fusion elementwise | flops 2097152 | bytes 25165824 | tf_op jit(solution)/shard_map/add | solution.py:49
  316.6 8.1 %fusion.4 = f32[512,64]{1,0:T(8,128)S(1)} fusion(f32[512,4096]{1,0:T(8,128)} %add.51, bf16[8192,256]{1,0:T(8,128)(2,1)} %copy-done.4, s32[]{:T(128)S(6)} %select_n.43, s32[]{:T(128)S(6)} %select_n.45), kind=kOutput, calls=%fused_computation.7 | convolution fusion | flops 1610612736 | bytes 9568264 | tf_op jit(solution)/shard_map/dot_general | solution.py:60
  325.8 3.2 constant_dynamic-slice_fusion.1
  329.0 55.7 %reduce-scatter.4.cloned.1.call-done = f32[32,64]{1,0:T(8,128)} async-done(((f32[256,64]{1,0:T(8,128)}), f32[32,64]{1,0:T(8,128)}) %reduce-scatter.4.cloned.1.call-update) | async-done | bytes 8208 | tf_op jit(solution)/shard_map/reduce_scatter | solution.py:75
  384.6 1.4 multiply_subtract_fusion
  (53 shorter events, 4.2 us)
Async XLA Ops:
  7.2 80.6 %copy-start = (bf16[1,512,512]{2,1,0:T(8,128)(2,1)S(1)}, bf16[1,512,512]{2,1,0:T(8,128)(2,1)}, u32[]{:S(2)}) copy-start(bf16[1,512,512]{2,1,0:T(8,128)(2,1)} %param.9) | copy-start | bytes 1572868
  7.2 80.6 %all-gather.2.cloned.1.call-start = ((), (), s32[]{:S(2)}) async-start(), calls=%async_computation.1 | async-start | bytes 4718592 | tf_op jit(solution)/shard_map/all_gather | solution.py:40
  7.9 376.7 %reduce-scatter.4.cloned.1.call-start = ((), (), s32[]{:S(2)}) async-start(), calls=%async_computation.2 | async-start | bytes 147456 | tf_op jit(solution)/shard_map/reduce_scatter | solution.py:75
  94.8 3.2 copy-start.2
  98.0 26.0 %copy-start.5 = (bf16[512,256]{1,0:T(8,128)(2,1)S(1)}, bf16[512,256]{1,0:T(8,128)(2,1)}, u32[]{:S(2)}) copy-start(bf16[512,256]{1,0:T(8,128)(2,1)} %param.11) | copy-start | bytes 786436
  98.0 73.9 %copy-start.8 = (s32[2]{0:T(128)S(1)}, s32[2]{0:T(128)}, u32[]{:S(2)}) copy-start(s32[2]{0:T(128)} %param.15) | copy-start | bytes 28
  98.0 73.9 %copy-start.6 = (s32[512]{0:T(512)S(1)}, s32[512]{0:T(512)}, u32[]{:S(2)}) copy-start(s32[512]{0:T(512)} %param.12) | copy-start | bytes 6148
  98.1 84.1 %copy-start.3 = (f32[512,512]{1,0:T(8,128)S(1)}, f32[512,512]{1,0:T(8,128)}, u32[]{:S(2)}) copy-start(f32[512,512]{1,0:T(8,128)} %param.13) | copy-start | bytes 3145732
  98.1 13.4 %collective-permute-start = (f32[512,4096]{1,0:T(8,128)S(1)}, f32[512,4096]{1,0:T(8,128)}, u32[]{:S(2)}, u32[]{:S(2)}) collective-permute-start(f32[512,4096]{1,0:T(8,128)S(1)} %bitcast_subtract_fusion), channel_id=1, source_target_pairs={{0,8},{8,0},{16,24},{24,16},{1,9},{9,1},{17,25},{25,17},{2,10},{10... | collective-permute-start | bytes 25165832 | tf_op jit(solution)/shard_map/ppermute | solution.py:17
  122.6 182.8 %collective-permute-start.1 = (f32[512,4096]{1,0:T(8,128)}, f32[512,4096]{1,0:T(8,128)}, u32[]{:S(2)}, u32[]{:S(2)}) collective-permute-start(f32[512,4096]{1,0:T(8,128)} %add.50), channel_id=1, source_target_pairs={{0,16},{16,0},{8,24},{24,8},{1,17},{17,1},{9,25},{25,9},{2,18},{18... | collective-permute-start | bytes 25165832 | tf_op jit(solution)/shard_map/ppermute | solution.py:17
  124.1 10.8 %collective-permute-start.2 = (bf16[512,256]{1,0:T(8,128)(2,1)S(1)}, bf16[512,256]{1,0:T(8,128)(2,1)S(1)}, u32[]{:S(2)}, u32[]{:S(2)}) collective-permute-start(bf16[512,256]{1,0:T(8,128)(2,1)S(1)} %copy-done.5), channel_id=1, source_target_pairs={{0,1},{1,2},{2,3},{3,4},{4,5},{5,6},{6,7},{7,0},{8,9},{9,10},{10,1... | collective-permute-start | bytes 786440 | tf_op jit(solution)/shard_map/ppermute | solution.py:54
  134.8 9.9 %collective-permute-start.3 = (bf16[512,256]{1,0:T(8,128)(2,1)S(1)}, bf16[512,256]{1,0:T(8,128)(2,1)S(1)}, u32[]{:S(2)}, u32[]{:S(2)}) collective-permute-start(bf16[512,256]{1,0:T(8,128)(2,1)S(1)} %collective-permute-done.2), channel_id=1, source_target_pairs={{0,1},{1,2},{2,3},{3,4},{4,5},{5,6},{6,7},{7,0},{8,9},{9,10},{10,1... | collective-permute-start | bytes 786440 | tf_op jit(solution)/shard_map/ppermute | solution.py:54
  144.7 9.1 %collective-permute-start.4 = (bf16[512,256]{1,0:T(8,128)(2,1)S(1)}, bf16[512,256]{1,0:T(8,128)(2,1)S(1)}, u32[]{:S(2)}, u32[]{:S(2)}) collective-permute-start(bf16[512,256]{1,0:T(8,128)(2,1)S(1)} %collective-permute-done.3), channel_id=1, source_target_pairs={{0,1},{1,2},{2,3},{3,4},{4,5},{5,6},{6,7},{7,0},{8,9},{9,10},{10,1... | collective-permute-start | bytes 786440 | tf_op jit(solution)/shard_map/ppermute | solution.py:54
  153.8 9.1 %collective-permute-start.5 = (bf16[512,256]{1,0:T(8,128)(2,1)S(1)}, bf16[512,256]{1,0:T(8,128)(2,1)S(1)}, u32[]{:S(2)}, u32[]{:S(2)}) collective-permute-start(bf16[512,256]{1,0:T(8,128)(2,1)S(1)} %collective-permute-done.4), channel_id=1, source_target_pairs={{0,1},{1,2},{2,3},{3,4},{4,5},{5,6},{6,7},{7,0},{8,9},{9,10},{10,1... | collective-permute-start | bytes 786440 | tf_op jit(solution)/shard_map/ppermute | solution.py:54
  162.9 9.1 %collective-permute-start.6 = (bf16[512,256]{1,0:T(8,128)(2,1)S(1)}, bf16[512,256]{1,0:T(8,128)(2,1)S(1)}, u32[]{:S(2)}, u32[]{:S(2)}) collective-permute-start(bf16[512,256]{1,0:T(8,128)(2,1)S(1)} %collective-permute-done.5), channel_id=1, source_target_pairs={{0,1},{1,2},{2,3},{3,4},{4,5},{5,6},{6,7},{7,0},{8,9},{9,10},{10,1... | collective-permute-start | bytes 786440 | tf_op jit(solution)/shard_map/ppermute | solution.py:54
  172.0 10.2 %collective-permute-start.7 = (bf16[512,256]{1,0:T(8,128)(2,1)S(1)}, bf16[512,256]{1,0:T(8,128)(2,1)S(1)}, u32[]{:S(2)}, u32[]{:S(2)}) collective-permute-start(bf16[512,256]{1,0:T(8,128)(2,1)S(1)} %collective-permute-done.6), channel_id=1, source_target_pairs={{0,1},{1,2},{2,3},{3,4},{4,5},{5,6},{6,7},{7,0},{8,9},{9,10},{10,1... | collective-permute-start | bytes 786440 | tf_op jit(solution)/shard_map/ppermute | solution.py:54
  182.1 9.1 %collective-permute-start.8 = (bf16[512,256]{1,0:T(8,128)(2,1)S(1)}, bf16[512,256]{1,0:T(8,128)(2,1)S(1)}, u32[]{:S(2)}, u32[]{:S(2)}) collective-permute-start(bf16[512,256]{1,0:T(8,128)(2,1)S(1)} %collective-permute-done.7), channel_id=1, source_target_pairs={{0,1},{1,2},{2,3},{3,4},{4,5},{5,6},{6,7},{7,0},{8,9},{9,10},{10,1... | collective-permute-start | bytes 786440 | tf_op jit(solution)/shard_map/ppermute | solution.py:54
  191.6 4.3 %copy-start.7 = (f32[512]{0:T(512)S(1)}, f32[512]{0:T(512)}, u32[]{:S(2)}) copy-start(f32[512]{0:T(512)} %param.14) | copy-start | bytes 6148
  191.6 1.9 copy-start.4
  316.6 69.5 %copy-start.1 = (bf16[1,512,512]{2,1,0:T(8,128)(2,1)S(1)}, bf16[1,512,512]{2,1,0:T(8,128)(2,1)}, u32[]{:S(2)}) copy-start(bf16[1,512,512]{2,1,0:T(8,128)(2,1)} %param.9) | copy-start | bytes 1572868
Sparse Core Ops, SparseCore 0:
  10.1 77.7 all-gather.1
  325.9 58.6 reduce-scatter.3
